TPU v7x, 32 devices: a whole 2x2x4 slice. The times are simulated.
32 devices in a mesh: row: 4 (over y, core), col: 8 (over z, x).
Axes of the slice: x: 2, y: 2, z: 4, core: 2. Of those that a mesh axis runs over, the one named last changes fastest.
Arguments:
- couplings: float32 [24576, 24576], P('row', 'col'), may hold values from -0.0390625 to 0.0390625
- diag_terms: float32 [24576], P('col'), may hold values from 1 to 4
- start_block: float32 [3, 24576], P(None, 'col'), may hold values from -6 to 6
Outputs:
- basis_scaled: float32 [2, 3, 24576], P(None, None, 'col')
- coeffs: float32 [2, 2, 3, 3], replicated
All inputs are finite; a program needn't handle non-finite values.
Results may differ from a plain program's by a relative error of at most 0.0003.
Values sent between devices are 32-bit elements; how exact they have to be, the bound alone decides.
A program may use at most 128 MiB of HBM per device.

v0:
```python
import jax
import jax.numpy as jnp
from jax import lax
from jax.sharding import PartitionSpec as P

ITERS = 2
M = 24576


def product(a, b):
    return jnp.dot(a, b, precision=lax.Precision.HIGHEST, preferred_element_type=jnp.float32)


def product_rows(a, matrix):
    return lax.dot_general(
        a,
        matrix,
        (((1,), (1,)), ((), ())),
        precision=lax.Precision.HIGHEST,
        preferred_element_type=jnp.float32,
    )


def shards(couplings, diag_terms, start_block):
    row_index = lax.axis_index("row")
    col_index = lax.axis_index("col")
    width_row = couplings.shape[0]
    width_col = couplings.shape[1]
    root = jnp.sqrt(jnp.float32(M))
    scaled = []
    blocks = []
    start_full, diag_full = (
        lax.all_gather(start_block, "col", axis=1, tiled=True),
        lax.all_gather(diag_terms, "col", axis=0, tiled=True),
    )
    first_factor = jnp.linalg.cholesky(product(start_full, start_full.T))
    current = jax.scipy.linalg.solve_triangular(first_factor, start_full, lower=True)
    basis = [current]
    for step in range(ITERS):
        col_piece = lax.dynamic_slice_in_dim(current, col_index * width_col, width_col, 1)
        row_piece = lax.dynamic_slice_in_dim(current, row_index * width_row, width_row, 1)
        forward_rows = lax.psum(product_rows(col_piece, couplings), "col")
        backward_cols = lax.psum(product(row_piece, couplings), "row")
        forward = lax.all_gather(forward_rows, "row", axis=1, tiled=True)
        backward = lax.all_gather(backward_cols, "col", axis=1, tiled=True)
        image = diag_full[None, :] * current + 0.5 * (forward + backward)
        prior = jnp.concatenate(basis, 0)
        correlation = product(image, prior.T)
        image = image - product(correlation, prior)
        factor = jnp.linalg.cholesky(product(image, image.T))
        current = jax.scipy.linalg.solve_triangular(factor, image, lower=True)
        basis.append(current)
        own_cols = lax.dynamic_slice_in_dim(current, col_index * width_col, width_col, 1)
        scaled.append(own_cols * root)
        blocks.append(jnp.stack([correlation[:, 3 * step : 3 * step + 3], factor]))
    return (jnp.stack(scaled), jnp.stack(blocks))


def solution(mesh):
    placed = (P("row", "col"), P("col"), P(None, "col"))
    return jax.shard_map(
        shards, mesh=mesh, in_specs=placed, out_specs=(P(None, None, "col"), P()), check_vma=False
    )
```

profile of v0, /device:TPU:0, one launch (start us, length us, event | category | flops | bytes accessed | tf_op | source)
XLA Modules:
  0.0 440.4 jit_solution(13411087968809847416)
XLA Ops:
  7.2 33.0 %all_gather.19 = f32[3,24576]{1,0:T(4,128)S(1)} all-gather(f32[3,3072]{1,0:T(4,128)} %param.8), channel_id=1, replica_groups=mesh['row'=4,'col'=8] {'col'}, dimensions={1}, use_global_device_ids=true | all-gather | bytes 331776 | tf_op jit(solution)/shard_map/all_gather | solution.py:33
  40.2 1.8 fusion.37
  42.1 0.3 cholesky.59
  42.4 0.6 compare_reduce_fusion.2
  43.1 0.6 fusion.14
  44.0 1.0 fusion.19
  45.0 66.2 %fusion.10 = f32[3,6144]{1,0:T(4,128)} fusion(f32[6144,3072]{1,0:T(8,128)} %param.6, f32[3,24576]{1,0:T(4,128)S(1)} %fusion.19, s32[]{:T(128)S(6)} %select_n.7), kind=kOutput, calls=%fused_computation.18 | convolution fusion | flops 679477248 | bytes 75620352 | tf_op jit(solution)/shard_map/dot_general | solution.py:15
  111.5 40.5 %fusion.8 = f32[3,3072]{1,0:T(4,128)S(1)} fusion(f32[6144,3072]{1,0:T(8,128)} %param.6, f32[3,24576]{1,0:T(4,128)S(1)} %fusion.19, s32[]{:T(128)S(6)} %select_n.14), kind=kOutput, calls=%fused_computation.14 | convolution fusion | flops 679477248 | bytes 75632640 | tf_op jit(solution)/shard_map/dot_general | solution.py:11
  152.0 10.9 %psum.29 = f32[3,3072]{1,0:T(4,128)S(1)} all-reduce(f32[3,3072]{1,0:T(4,128)S(1)} %fusion.8), channel_id=1, replica_groups=mesh['row'=4,'col'=8] {'row'}, use_global_device_ids=true, to_apply=%region_3.0 | all-reduce | flops 9216 | bytes 73728 | tf_op jit(solution)/shard_map/psum | solution.py:43
  162.9 31.0 %all_gather.21 = f32[3,24576]{1,0:T(4,128)S(1)} all-gather(f32[3,3072]{1,0:T(4,128)S(1)} %psum.29), channel_id=1, replica_groups=mesh['row'=4,'col'=8] {'col'}, dimensions={1}, use_global_device_ids=true | all-gather | bytes 331776 | tf_op jit(solution)/shard_map/all_gather | solution.py:45
  193.9 30.6 %all_gather.18 = f32[24576]{0:T(1024)S(1)} all-gather(f32[3072]{0:T(1024)S(1)} %copy-done), channel_id=1, replica_groups=mesh['row'=4,'col'=8] {'col'}, dimensions={0}, use_global_device_ids=true | all-gather | bytes 110592 | tf_op jit(solution)/shard_map/all_gather | solution.py:34
  224.6 6.8 %all_gather.20 = f32[3,24576]{1,0:T(4,128)S(1)} all-gather(f32[3,6144]{1,0:T(4,128)} %all-reduce.3.cloned.1.call-done), channel_id=1, replica_groups=mesh['row'=4,'col'=8] {'row'}, dimensions={1}, use_global_device_ids=true | all-gather | bytes 368640 | tf_op jit(solution)/shard_map/all_gather | solution.py:44
  231.3 1.8 fusion.1
  233.1 0.9 convolution_subtract_fusion
  234.0 1.8 fusion.38
  236.3 0.6 compare_reduce_fusion.1
  236.9 0.6 fusion.27
  237.8 1.0 fusion.17
  238.8 66.5 %fusion.12 = f32[3,6144]{1,0:T(4,128)} fusion(f32[6144,3072]{1,0:T(8,128)} %param.6, f32[3,24576]{1,0:T(4,128)S(1)} %fusion.17, s32[]{:T(128)S(6)} %select_n.7), kind=kOutput, calls=%fused_computation.20 | convolution fusion | flops 679477248 | bytes 75620352 | tf_op jit(solution)/shard_map/dot_general | solution.py:15
  305.3 40.8 %fusion.6 = f32[3,3072]{1,0:T(4,128)S(1)} fusion(f32[6144,3072]{1,0:T(8,128)} %param.6, f32[3,24576]{1,0:T(4,128)S(1)} %fusion.17, s32[]{:T(128)S(6)} %select_n.14), kind=kOutput, calls=%fused_computation.12 | convolution fusion | flops 679477248 | bytes 75632640 | tf_op jit(solution)/shard_map/dot_general | solution.py:11
  346.1 11.9 %psum.31 = f32[3,3072]{1,0:T(4,128)S(1)} all-reduce(f32[3,3072]{1,0:T(4,128)S(1)} %fusion.6), channel_id=1, replica_groups=mesh['row'=4,'col'=8] {'row'}, use_global_device_ids=true, to_apply=%region_5.8 | all-reduce | flops 9216 | bytes 73728 | tf_op jit(solution)/shard_map/psum | solution.py:43
  358.0 31.2 %all_gather.23 = f32[3,24576]{1,0:T(4,128)S(1)} all-gather(f32[3,3072]{1,0:T(4,128)S(1)} %psum.31), channel_id=1, replica_groups=mesh['row'=4,'col'=8] {'col'}, dimensions={1}, use_global_device_ids=true | all-gather | bytes 331776 | tf_op jit(solution)/shard_map/all_gather | solution.py:45
  389.2 28.4 %all-reduce.5.cloned.1.call-done = f32[3,6144]{1,0:T(4,128)} async-done(((f32[3,6144]{1,0:T(4,128)}), f32[3,6144]{1,0:T(4,128)}) %all-reduce.5.cloned.1.call-update) | async-done | bytes 73744 | tf_op jit(solution)/shard_map/psum | solution.py:42
  417.6 6.6 %all_gather.22 = f32[3,24576]{1,0:T(4,128)S(1)} all-gather(f32[3,6144]{1,0:T(4,128)} %all-reduce.5.cloned.1.call-done), channel_id=1, replica_groups=mesh['row'=4,'col'=8] {'row'}, dimensions={1}, use_global_device_ids=true | all-gather | bytes 368640 | tf_op jit(solution)/shard_map/all_gather | solution.py:44
  424.2 1.8 fusion
  426.0 1.0 convolution_subtract_fusion.1
  427.0 1.8 fusion.39
  429.2 0.6 compare_reduce_fusion
  429.9 0.7 fusion.28
  430.8 1.0 fusion.15
  431.9 0.7 copy.22
  432.6 0.6 pad_maximum_fusion.4
  (28 shorter events, 2.2 us)
Async XLA Ops:
  7.2 217.4 %all-reduce.3.cloned.1.call-start = ((), (), s32[]{:S(2)}) async-start(), calls=%async_computation | async-start | bytes 196608 | tf_op jit(solution)/shard_map/psum | solution.py:42
  45.0 148.9 %copy-start = (f32[3072]{0:T(1024)S(1)}, f32[3072]{0:T(1024)}, u32[]{:S(2)}) copy-start(f32[3072]{0:T(1024)} %param.7) | copy-start | bytes 36868
  111.2 306.3 %all-reduce.5.cloned.1.call-start = ((), (), s32[]{:S(2)}) async-start(), calls=%async_computation.1 | async-start | bytes 196608 | tf_op jit(solution)/shard_map/psum | solution.py:42
Sparse Core Ops, SparseCore 0:
  111.4 71.3 all-reduce.2
  346.2 71.3 all-reduce.4
where the time goes:
time: 449 us; the launch traced here: 440 us
  matrix products  228 us (51%)
  blocking collectives  162 us (36%)
  waiting for transfers between devices  28.4 us (6%)
  between operations  14.6 us (3%)
  other arithmetic  6.39 us (1%)
    dot_general x2, matrix products, product_rows(): lax.dot_general(a, matrix, (((1,), (1,)), ((), ())), precision=lax.Precis...  133 us
    dot_general x9, matrix products, product(): jnp.dot(a, b, precision=lax.Precision.HIGHEST, preferred_element_type=jnp...  92.2 us
    all_gather x2, blocking collectives, shards(): backward = lax.all_gather(backward_cols, 'col', axis=1, tiled=True)  62.2 us
    all_gather x1, blocking collectives, shards(): lax.all_gather(start_block, 'col', axis=1, tiled=True)  33 us
    all_gather x1, blocking collectives, shards(): lax.all_gather(diag_terms, 'col', axis=0, tiled=True)  30.6 us
    psum x2, waiting for transfers between devices, shards(): forward_rows = lax.psum(product_rows(col_piece, couplings), 'col')  28.4 us
    psum x2, blocking collectives, shards(): backward_cols = lax.psum(product(row_piece, couplings), 'row')  22.8 us
    all_gather x2, blocking collectives, shards(): forward = lax.all_gather(forward_rows, 'row', axis=1, tiled=True)  13.4 us
  transfers between devices with their start and end apart: 2, of which 1 were waited for; matrix products, arithmetic and copies ran while one was open for 9% of the time, Pallas kernels for 0%

commit v1 on v0

v1 whole, which is shorter than its diff:
```python
import functools

import jax
import jax.numpy as jnp
from jax import lax
from jax.experimental import pallas as pl
from jax.experimental.pallas import tpu as pltpu
from jax.sharding import PartitionSpec as P

ITERS = 2
LANES = 128
CONTRACT_LAST = (((1,), (1,)), ((), ()))
CONTRACT_FIRST = (((1,), (0,)), ((), ()))


def split(rows):
    high = lax.reduce_precision(rows, 8, 7)
    low = rows - high
    stacked = jnp.concatenate([high, low], 0).astype(jnp.bfloat16)
    return jnp.pad(stacked, ((0, 16 - stacked.shape[0]), (0, 0)))


def both_kernel(col_ref, row_ref, g_ref, forward_ref, backward_ref):
    g = g_ref[...]
    high = g.astype(jnp.bfloat16)
    low = (g - high.astype(jnp.float32)).astype(jnp.bfloat16)
    col = col_ref[...]
    row = row_ref[...]

    def product(a, b, dims):
        return lax.dot_general(a, b, dims, preferred_element_type=jnp.float32)

    forward_ref[...] = product(col, high, CONTRACT_LAST) + product(col, low, CONTRACT_LAST)

    @pl.when(pl.program_id(0) == 0)
    def _():
        backward_ref[...] = jnp.zeros_like(backward_ref)

    backward_ref[...] += product(row, high, CONTRACT_FIRST) + product(row, low, CONTRACT_FIRST)


def both_products(col_piece, row_piece, couplings):
    height, width = couplings.shape
    tile = min(512, height)
    forward, backward = pl.pallas_call(
        both_kernel,
        grid=(height // tile,),
        in_specs=[
            pl.BlockSpec((16, width), lambda i: (0, 0)),
            pl.BlockSpec((16, tile), lambda i: (0, i)),
            pl.BlockSpec((tile, width), lambda i: (i, 0)),
        ],
        out_specs=[
            pl.BlockSpec((16, tile), lambda i: (0, i)),
            pl.BlockSpec((16, width), lambda i: (0, 0)),
        ],
        out_shape=[
            jax.ShapeDtypeStruct((16, height), jnp.float32),
            jax.ShapeDtypeStruct((16, width), jnp.float32),
        ],
        compiler_params=pltpu.CompilerParams(
            dimension_semantics=("arbitrary",), vmem_limit_bytes=56 * 1024 * 1024
        ),
    )(split(col_piece), split(row_piece), couplings)
    return forward[0:3] + forward[3:6], backward[0:3] + backward[3:6]


def total(x):
    return jnp.sum(jnp.sum(x, axis=0, keepdims=True), axis=1, keepdims=True)


def ortho_kernel(step, *refs):
    if step < 0:
        image_ref, new_ref = refs
        image = [image_ref[i] for i in range(3)]
    else:
        raw_ref, diag_ref = refs[0], refs[1]
        prior_refs = refs[2 : 3 + step]
        new_ref, small_ref = refs[3 + step :]
        diag = diag_ref[...]
        image = [diag * prior_refs[step][i] + raw_ref[i] for i in range(3)]
        row_id = lax.broadcasted_iota(jnp.int32, small_ref.shape, 0)
        col_id = lax.broadcasted_iota(jnp.int32, small_ref.shape, 1)
        small = jnp.zeros(small_ref.shape, jnp.float32)
        taken = list(image)
        for b, prior_ref in enumerate(prior_refs):
            for j in range(3):
                row = prior_ref[j]
                for i in range(3):
                    value = total(image[i] * row)
                    taken[i] = taken[i] - value * row
                    if b == step:
                        small = jnp.where((row_id == i) & (col_id == j), value, small)
        image = taken
    factor = [[None] * 3 for _ in range(3)]
    for i in range(3):
        for j in range(i + 1):
            value = total(image[i] * image[j])
            for k in range(j):
                value = value - factor[i][k] * factor[j][k]
            factor[i][j] = jnp.sqrt(value) if i == j else value / factor[j][j]
            if step >= 0:
                small = jnp.where((row_id == i) & (col_id == j + 3), factor[i][j], small)
    done = []
    for i in range(3):
        row = image[i]
        for k in range(i):
            row = row - factor[i][k] * done[k]
        row = row / factor[i][i]
        done.append(row)
        new_ref[i] = row
    if step >= 0:
        small_ref[...] = small


def ortho(step, *arrays):
    shapes = [jax.ShapeDtypeStruct(arrays[0].shape, jnp.float32)]
    if step >= 0:
        shapes.append(jax.ShapeDtypeStruct((8, LANES), jnp.float32))
    return pl.pallas_call(
        functools.partial(ortho_kernel, step),
        in_specs=[pl.BlockSpec(memory_space=pltpu.VMEM)] * len(arrays),
        out_specs=[pl.BlockSpec(memory_space=pltpu.VMEM)] * len(shapes),
        out_shape=shapes,
        compiler_params=pltpu.CompilerParams(vmem_limit_bytes=32 * 1024 * 1024),
    )(*arrays)


def shards(couplings, diag_terms, start_block):
    row_index = lax.axis_index("row")
    col_index = lax.axis_index("col")
    height, width = couplings.shape
    lines_row, lines_col = height // LANES, width // LANES
    modes = width * lax.axis_size("col")
    lines = modes // LANES
    root = jnp.sqrt(jnp.float32(modes))
    own = jnp.concatenate([start_block, diag_terms[None, :]], 0).reshape(4, lines_col, LANES)
    full = lax.all_gather(own, "col", axis=1, tiled=True)
    diag = full[3]
    (current,) = ortho(-1, full[:3])
    basis = [current]
    scaled = []
    blocks = []
    for step in range(ITERS):
        col_piece = lax.dynamic_slice_in_dim(current, col_index * lines_col, lines_col, 1)
        row_piece = lax.dynamic_slice_in_dim(current, row_index * lines_row, lines_row, 1)
        forward, backward = both_products(
            col_piece.reshape(3, width), row_piece.reshape(3, height), couplings
        )
        placed_forward = lax.dynamic_update_slice_in_dim(
            jnp.zeros((3, lines, LANES), jnp.float32),
            (0.5 * forward).reshape(3, lines_row, LANES), row_index * lines_row, 1,
        )
        placed_backward = lax.dynamic_update_slice_in_dim(
            jnp.zeros((3, lines, LANES), jnp.float32),
            (0.5 * backward).reshape(3, lines_col, LANES), col_index * lines_col, 1,
        )
        raw = lax.psum(placed_forward + placed_backward, ("row", "col"))
        current, small = ortho(step, raw, diag, *basis)
        basis.append(current)
        own_cols = lax.dynamic_slice_in_dim(current, col_index * lines_col, lines_col, 1)
        scaled.append(own_cols.reshape(3, width) * root)
        blocks.append(jnp.stack([small[:3, 0:3], small[:3, 3:6]]))
    return (jnp.stack(scaled), jnp.stack(blocks))


def solution(mesh):
    placed = (P("row", "col"), P("col"), P(None, "col"))
    return jax.shard_map(
        shards, mesh=mesh, in_specs=placed, out_specs=(P(None, None, "col"), P()), check_vma=False
    )
```

time: 449 us -> 392 us (0.87); the launches traced: 440 us -> 390 us
  matrix products: 228 us -> 0 us
  waiting for transfers between devices: 28.4 us -> 256 us
  blocking collectives: 162 us -> 32.8 us
  Pallas kernels: 0 us -> 73.6 us
    psum x2, waiting for transfers between devices: 28.4 us -> 256 us  [shards(): raw = lax.psum(placed_forward + placed_backward, ('row', 'col'))]
    dot_general x11 -> x0, matrix products: 225 us -> none  [the longest x2 133 us: product_rows(): lax.dot_general(a, matrix, (((1,), (1,)), ((), ())), precision=lax.Precis...]
    all_gather x6 -> x1, blocking collectives: 139 us -> 32.8 us  [shards(): full = lax.all_gather(own, 'col', axis=1, tiled=True)]
    pallas_call x0 -> x5, Pallas kernels: none -> 73.6 us  [the longest x2 72.6 us: both_products(): pl.pallas_call(both_kernel, grid=(height // tile,), in_specs=[pl.BlockSpe...]
    psum x2 -> x0, blocking collectives: 22.8 us -> none  [shards(): backward_cols = lax.psum(product(row_piece, couplings), 'row')]
    another operation x17 -> x6, other arithmetic: 5.71 us -> 0.16 us  [the longest x6 1.93 us: shards(): factor = jnp.linalg.cholesky(product(image, image.T))]
  transfers between devices with their start and end apart: 2 -> 2, of which waited for: 1 -> 2; matrix products, arithmetic and copies ran while one was open for 9% -> 0% of each run, Pallas kernels for 0% -> 0%
where the time goes in v1:
time: 392 us; the launch traced here: 390 us
  waiting for transfers between devices  256 us (65%)
  Pallas kernels  73.6 us (19%)
  blocking collectives  32.8 us (8%)
  between operations  14.2 us (4%)
  other arithmetic  8.45 us (2%)
  local copies, waits for them, and re-layouts  5.14 us (1%)
    psum x2, waiting for transfers between devices, shards(): raw = lax.psum(placed_forward + placed_backward, ('row', 'col'))  256 us
    pallas_call x2, Pallas kernels, both_products(): pl.pallas_call(both_kernel, grid=(height // tile,), in_specs=[pl.BlockSpe...  72.6 us
    all_gather x1, blocking collectives, shards(): full = lax.all_gather(own, 'col', axis=1, tiled=True)  32.8 us
  transfers between devices with their start and end apart: 2, of which 2 were waited for; matrix products, arithmetic and copies ran while one was open for 0% of the time, Pallas kernels for 0%

profile of v1, /device:TPU:0, one launch (start us, length us, event | category | flops | bytes accessed | tf_op | source)
XLA Modules:
  0.0 390.4 jit_solution(15667515373319080841)
XLA Ops:
  7.2 0.0 all-reduce.7.cloned.1.call-start
  7.2 0.8 copy.36
  8.0 0.7 pad_maximum_fusion.1
  8.7 32.8 %all_gather.3 = f32[4,192,128]{2,1,0:T(8,128)S(1)} all-gather(f32[4,24,128]{2,1,0:T(8,128)S(1)} %pad_maximum_fusion.1), channel_id=1, replica_groups=mesh['row'=4,'col'=8] {'col'}, dimensions={1}, use_global_device_ids=true | all-gather | bytes 442368 | tf_op jit(solution)/shard_map/all_gather | solution.py:138
  41.5 0.2 shard_map.50.refs_2_
  41.8 0.1 reduce-precision_convert_fusion.1
  41.8 0.7 fusion.12.col_ref
  42.5 0.7 fusion.4.row_ref
  43.2 36.3 %shard_map.51 = (f32[16,6144]{1,0:T(8,128)}, f32[16,3072]{1,0:T(8,128)}) custom-call(bf16[16,3072]{1,0:T(8,128)(2,1)} %fusion.12.col_ref, bf16[16,6144]{1,0:T(8,128)(2,1)} %fusion.4.row_ref, f32[6144,3072]{1,0:T(8,128)} %g_ref.3), custom_call_target="tpu_custom_call" | custom-call | tf_op jit(solution)/shard_map/pallas_call | solution.py:45
  79.6 1.1 multiply_bitcast_fusion.1
  80.6 1.0 multiply_bitcast_fusion.3
  81.7 0.7 copy-done.3
  82.4 0.0 all-reduce.7.cloned.1.call-update
  82.4 0.0 all-reduce.9.cloned.1.call-start
  82.5 128.2 %all-reduce.7.cloned.1.call-done.refs_0_ = f32[3,192,128]{2,1,0:T(8,128)} async-done(((f32[3,192,128]{2,1,0:T(8,128)}), f32[3,192,128]{2,1,0:T(8,128)}) %all-reduce.7.cloned.1.call-update) | async-done | bytes 294928 | tf_op jit(solution)/shard_map/psum | solution.py:158
  210.6 1.0 copy-done.1
  211.6 0.3 shard_map.52
  212.0 0.1 reduce-precision_convert_fusion
  212.1 0.7 fusion.5.row_ref
  212.8 0.7 fusion.13.col_ref
  213.5 36.3 %shard_map.53 = (f32[16,6144]{1,0:T(8,128)}, f32[16,3072]{1,0:T(8,128)}) custom-call(bf16[16,3072]{1,0:T(8,128)(2,1)} %fusion.13.col_ref, bf16[16,6144]{1,0:T(8,128)(2,1)} %fusion.5.row_ref, f32[6144,3072]{1,0:T(8,128)} %g_ref.3), custom_call_target="tpu_custom_call" | custom-call | tf_op jit(solution)/shard_map/pallas_call | solution.py:45
  249.8 1.1 multiply_bitcast_fusion
  250.9 1.0 multiply_bitcast_fusion.2
  251.9 0.7 copy-done.2
  252.6 0.0 all-reduce.9.cloned.1.call-update
  252.7 0.1 slice_bitcast_fusion.4
  252.8 127.9 %all-reduce.9.cloned.1.call-done.refs_0_ = f32[3,192,128]{2,1,0:T(8,128)} async-done(((f32[3,192,128]{2,1,0:T(8,128)}), f32[3,192,128]{2,1,0:T(8,128)}) %all-reduce.9.cloned.1.call-update) | async-done | bytes 294928 | tf_op jit(solution)/shard_map/psum | solution.py:158
  380.7 1.0 copy-done
  381.7 0.5 shard_map.54
  382.2 0.1 slice_bitcast_fusion.2
  382.3 0.7 copy.11
  383.0 0.6 pad_maximum_fusion.2
  (25 shorter events, 0.3 us)
Async XLA Ops:
  7.2 203.5 %all-reduce.7.cloned.1.call-start = ((), (), s32[]{:S(2)}) async-start(), calls=%async_computation | async-start | bytes 589824 | tf_op jit(solution)/shard_map/psum | solution.py:158
  81.7 0.7 copy-start.3
  82.4 298.3 %all-reduce.9.cloned.1.call-start = ((), (), s32[]{:S(2)}) async-start(), calls=%async_computation.1 | async-start | bytes 589824 | tf_op jit(solution)/shard_map/psum | solution.py:158
  210.6 1.0 copy-start.1
  251.9 0.7 copy-start.2
  380.7 1.0 copy-start
Sparse Core Ops, SparseCore 0:
  82.5 128.0 all-reduce.6
  252.8 127.8 all-reduce.8
